TPU v7x, 256 devices: a whole 4x4x8 slice. The times are simulated.
256 devices in a mesh: dp: 4 (over x), group: 4 (over y), member: 16 (over z, core).
Axes of the slice: x: 4, y: 4, z: 8, core: 2. Of those that a mesh axis runs over, the one named last changes fastest.
Arguments:
- tokens: bfloat16 [2048, 2880], P(('dp', 'group', 'member')), may hold values from -6 to 6
- cotangent: bfloat16 [2048, 2880], P(('dp', 'group', 'member')), may hold values from -6 to 6
- expert_ids: int32 [2048, 4], P(('dp', 'group', 'member')), may hold values from 0 to 7, all different within a row; in each aligned block of 8 rows (0 to 7, 8 to 15, ...) at most 8 rows name the same one
- gate_weights: float32 [2048, 4], P(('dp', 'group', 'member')), may hold values from 0.25 to 1
- w_gate: bfloat16 [8, 2880, 2880], P('group', 'member'), may hold values from -0.109375 to 0.109375
- w_up: bfloat16 [8, 2880, 2880], P('group', 'member'), may hold values from -0.109375 to 0.109375
- w_down: bfloat16 [8, 2880, 2880], P('group', 'member'), may hold values from -0.109375 to 0.109375
Outputs:
- grad_tokens: bfloat16 [2048, 2880], P(('dp', 'group', 'member'))
- grad_gate: bfloat16 [8, 2880, 2880], P('group', 'member', 'dp')
- grad_up: bfloat16 [8, 2880, 2880], P('group', 'member', 'dp')
- grad_down: bfloat16 [8, 2880, 2880], P('group', 'member', 'dp')
Inputs may be any that keep to these rules, and one draw needn't show every extreme that they name: `expert_ids`: each row names 4 different experts. Among the rows of one device no expert is named by more than 8 rows, a bound that some block reaches of them.
All inputs are finite; a program needn't handle non-finite values.
Results may differ from a plain program's by a relative error of at most 0.02.
Values may be sent and summed in bfloat16 or wider, within the bound.
No kernel may reach another device: no remote copies, remote signals or barrier semaphores. Data moves between devices by JAX's collectives and lax.ppermute only.
A program may use at most 128 MiB of HBM per device.

v0:
```python
import jax
import jax.numpy as jnp
from jax import lax
from jax.sharding import PartitionSpec as P


def on_device(tokens, cotangent, expert_ids, gate_weights, w_gate, w_up, w_down):
    n_group = lax.axis_size("group")
    n_member = lax.axis_size("member")
    local_experts = w_gate.shape[0]
    experts = local_experts * n_group
    tok_rows = tokens.shape[0]
    top_count = expert_ids.shape[1]
    model_width = tokens.shape[1]
    capacity = 2 * tok_rows * top_count // experts
    slot_block = local_experts * capacity
    flat_ids = expert_ids.reshape(-1)
    picked = (flat_ids[:, None] == jnp.arange(experts, dtype=jnp.int32)[None, :]).astype(jnp.int32)
    before = jnp.cumsum(picked, axis=0) - picked
    slot_index = jnp.sum(before * picked, axis=1)
    target = flat_ids * capacity + slot_index
    target_hot = (
        target[:, None] == jnp.arange(experts * capacity, dtype=jnp.int32)[None, :]
    ).astype(jnp.float32)
    owner_index = jnp.arange(tok_rows * top_count, dtype=jnp.int32) // top_count
    owner_hot = (owner_index[:, None] == jnp.arange(tok_rows, dtype=jnp.int32)[None, :]).astype(
        jnp.float32
    )
    placing = jnp.dot(target_hot.T, owner_hot, precision=lax.Precision.HIGHEST)
    weighted = jnp.dot(
        (target_hot * gate_weights.reshape(-1)[:, None]).T,
        owner_hot,
        precision=lax.Precision.HIGHEST,
    )
    sent_inputs = jnp.dot(
        placing.astype(jnp.bfloat16), tokens, preferred_element_type=jnp.float32
    ).astype(jnp.bfloat16)
    sent_scaled = jnp.dot(
        weighted, cotangent.astype(jnp.float32), precision=lax.Precision.HIGHEST
    ).astype(jnp.bfloat16)
    outgoing = jnp.stack([sent_inputs, sent_scaled])
    landed = lax.all_to_all(
        outgoing.reshape(2, n_group, slot_block, model_width),
        "group",
        split_axis=1,
        concat_axis=1,
        tiled=True,
    )
    arrived = lax.all_gather(
        landed.reshape(2, 1, n_group, slot_block, model_width), "member", axis=1, tiled=True
    )
    arrived_data = arrived.reshape(2, n_member * n_group, local_experts, capacity, model_width)
    inputs_rows = arrived_data[0]
    scaled_rows = arrived_data[1]
    gate_pre = jnp.einsum("rjcd,jhd->rjch", inputs_rows, w_gate, preferred_element_type=jnp.float32)
    up_pre = jnp.einsum("rjcd,jhd->rjch", inputs_rows, w_up, preferred_element_type=jnp.float32)
    sigmoid_gate = jax.nn.sigmoid(gate_pre)
    hidden = (gate_pre * sigmoid_gate * up_pre).astype(jnp.bfloat16)
    grad_hidden = jnp.einsum(
        "rjcd,jhd->rjch", scaled_rows, w_down, preferred_element_type=jnp.float32
    )
    grad_up_pre = (grad_hidden * gate_pre * sigmoid_gate).astype(jnp.bfloat16)
    grad_gate_pre = (
        grad_hidden * up_pre * sigmoid_gate * (1.0 + gate_pre * (1.0 - sigmoid_gate))
    ).astype(jnp.bfloat16)
    weight_gate = jnp.einsum(
        "rjch,rjcd->jhd", grad_gate_pre, inputs_rows, preferred_element_type=jnp.float32
    )
    weight_up = jnp.einsum(
        "rjch,rjcd->jhd", grad_up_pre, inputs_rows, preferred_element_type=jnp.float32
    )
    weight_down = jnp.einsum(
        "rjch,rjcd->jhd", hidden, scaled_rows, preferred_element_type=jnp.float32
    )
    own_rows = n_group * slot_block
    summed = jnp.einsum("rjch,jhd->rjcd", grad_gate_pre, w_gate, preferred_element_type=jnp.float32)
    summed = summed + jnp.einsum(
        "rjch,jhd->rjcd", grad_up_pre, w_up, preferred_element_type=jnp.float32
    )
    reduced = lax.psum_scatter(
        summed.reshape(lax.axis_size("member") * own_rows, model_width).astype(jnp.bfloat16),
        "member",
        scatter_dimension=0,
        tiled=True,
    )
    mine = reduced.reshape(n_group, slot_block, model_width)
    returned = lax.all_to_all(mine, "group", split_axis=0, concat_axis=0, tiled=True).reshape(
        experts * capacity, model_width
    )
    grad_tokens = jnp.dot(
        placing.T.astype(jnp.bfloat16), returned, preferred_element_type=jnp.float32
    ).astype(jnp.bfloat16)
    summed_weights = (
        lax.psum_scatter(
            weight_gate.astype(jnp.bfloat16), "dp", scatter_dimension=2, tiled=True
        ).astype(jnp.float32),
        lax.psum_scatter(
            weight_up.astype(jnp.bfloat16), "dp", scatter_dimension=2, tiled=True
        ).astype(jnp.float32),
        lax.psum_scatter(
            weight_down.astype(jnp.bfloat16), "dp", scatter_dimension=2, tiled=True
        ).astype(jnp.float32),
    )
    return (
        grad_tokens,
        summed_weights[0].astype(jnp.bfloat16),
        summed_weights[1].astype(jnp.bfloat16),
        summed_weights[2].astype(jnp.bfloat16),
    )


def solution(mesh):
    placed = (
        P(("dp", "group", "member"), None),
        P(("dp", "group", "member"), None),
        P(("dp", "group", "member"), None),
        P(("dp", "group", "member"), None),
        P("group", "member", None),
        P("group", "member", None),
        P("group", "member", None),
    )
    return jax.shard_map(
        on_device,
        mesh=mesh,
        in_specs=placed,
        out_specs=(
            P(("dp", "group", "member"), None),
            P("group", "member", "dp"),
            P("group", "member", "dp"),
            P("group", "member", "dp"),
        ),
        check_vma=False,
    )
```

profile of v0, /device:TPU:1, one launch (start us, length us, event | category | flops | bytes accessed | tf_op | source)
XLA Modules:
  0.0 319.9 jit_solution(6226053942061887606)
XLA Ops:
  7.2 0.0 copy-start
  7.2 0.0 all-gather.3.cloned.1.call-start
  7.2 0.9 copy.47
  8.1 0.1 reshape.55
  8.2 0.8 copy.48
  9.0 0.1 mul.50
  9.0 0.1 fusion.57
  9.1 0.1 reduce_window_sum.11
  9.2 0.2 select_reduce_fusion
  9.4 0.3 convolution_convert_fusion.3
  9.6 0.3 fusion.55
  9.9 1.3 convolution_convert_fusion
  11.2 1.1 convolution_convert_fusion.1
  12.3 0.1 pad_maximum_fusion
  12.4 15.9 %all_to_all.10 = bf16[2,4,16,2880]{3,2,0,1:T(8,128)(2,1)S(1)} all-to-all(bf16[2,4,16,2880]{3,2,0,1:T(8,128)(2,1)S(1)} %pad_maximum_fusion), channel_id=1, replica_groups=mesh['dp'=4,'group'=4,'member'=16] {'group'}, dimensions={1} | all-to-all | bytes 1474560 | tf_op jit(solution)/shard_map/all_to_all | solution.py:42
  28.3 0.9 copy.51
  29.2 0.0 all-gather.3.cloned.1.call-update
  29.2 0.0 reduce-scatter.11.cloned.1.call-start
  29.3 75.7 %all-gather.3.cloned.1.call-done = bf16[2,64,16,2880]{3,2,1,0:T(8,128)(2,1)} async-done(((bf16[2,4,16,2880]{3,2,1,0:T(8,128)(2,1)}), bf16[2,64,16,2880]{3,2,1,0:T(8,128)(2,1)}) %all-gather.3.cloned.1.call-update) | async-done | bytes 11796496 | tf_op jit(solution)/shard_map/all_gather | solution.py:49
  105.0 9.7 %slice_bitcast_fusion.1 = (bf16[64,2,8,2880]{3,2,1,0:T(8,128)(2,1)}, bf16[64,2,8,2880]{3,2,1,0:T(8,128)(2,1)}) fusion(bf16[2,64,16,2880]{3,2,1,0:T(8,128)(2,1)} %all-gather.3.cloned.1.call-done), kind=kLoop, calls=%fused_computation.2 | loop fusion | bytes 23592960 | tf_op jit(solution)/shard_map/squeeze | solution.py:54
  114.7 0.0 copy-start.2
  114.7 0.0 copy-start.3
  114.7 5.3 %fusion.47 = f32[64,2,8,180]{3,2,0,1:T(8,128)S(1)} fusion(bf16[2,180,2880,1]{2,0,1,3:T(2,128)(2,1)} %bitcast.70, bf16[64,2,8,2880]{3,2,1,0:T(8,128)(2,1)} %get-tuple-element.16), kind=kOutput, calls=%fused_computation.33 | convolution fusion | flops 1061683200 | bytes 8709120 | tf_op jit(solution)/shard_map/rjcd,jhd->rjch/dot_general | solution.py:59
  120.0 0.0 copy-done.2
  120.0 0.4 copy-done.3
  120.4 1.8 fusion.42
  122.2 0.0 copy-done
  122.2 3.0 multiply_convert_fusion
  125.2 1.8 fusion.32
  127.0 4.4 %fusion.12 = bf16[64,2,8,2880]{3,2,0,1:T(8,128)(2,1)} fusion(f32[2,64,8,2880]{3,2,1,0:T(8,128)S(1)} %fusion.32, bf16[64,2,8,180]{3,2,0,1:T(8,128)(2,1)S(1)} %get-tuple-element.20, bf16[2,180,2880,1]{2,0,1,3:T(2,128)(2,1)S(1)} %bitcast.56), kind=kOutput, calls=%fused_computation.15 | convolution fusion | flops 1067581440 | bytes 20136960 | tf_op jit(solution)/shard_map/rjch,jhd->rjcd/dot_general | solution.py:77
  131.4 5.7 %copy.60 = bf16[64,2,8,2880]{3,2,1,0:T(8,128)(2,1)} copy(bf16[64,2,8,2880]{3,2,0,1:T(8,128)(2,1)} %fusion.12) | data formatting | bytes 11796480 | tf_op jit(solution)/shard_map/convert_element_type | solution.py:81
  137.1 0.0 copy-start.4
  137.1 0.0 reduce-scatter.11.cloned.1.call-update
  137.2 0.2 reduce-scatter.17.cloned.1.call-start
  137.4 0.8 copy-done.4
  138.2 5.5 %fusion.22 = bf16[2,180,2880]{2,1,0:T(8,128)(2,1)} fusion(bf16[64,2,8,2880]{3,2,1,0:T(8,128)(2,1)} %get-tuple-element.16, bf16[64,2,8,180]{3,2,0,1:T(8,128)(2,1)S(1)} %copy-done.4), kind=kOutput, calls=%fused_computation.19 | convolution fusion | flops 1062720000 | bytes 8340480 | tf_op jit(solution)/shard_map/rjch,rjcd->jhd/dot_general | solution.py:72
  143.7 8.4 %copy.92 = bf16[2,180,2880]{1,0,2:T(2,128)(2,1)} copy(bf16[2,180,2880]{2,1,0:T(8,128)(2,1)} %fusion.22) | data formatting | bytes 4147200
  152.2 7.4 %reshape.76 = bf16[2880,360]{1,0:T(8,128)(2,1)} reshape(bf16[2880,2,180]{2,1,0:T(2,128)(2,1)} %bitcast.58) | data formatting | bytes 4147200
  159.6 0.0 reduce-scatter.17.cloned.1.call-update
  159.6 0.0 reduce-scatter.15.cloned.1.call-start
  159.7 5.6 %fusion.25 = bf16[2,180,2880]{2,1,0:T(8,128)(2,1)} fusion(bf16[64,2,8,2880]{3,2,1,0:T(8,128)(2,1)} %get-tuple-element.17, bf16[64,2,8,180]{3,2,0,1:T(8,128)(2,1)S(1)} %get-tuple-element.20), kind=kOutput, calls=%fused_computation.20 | convolution fusion | flops 1062720000 | bytes 8340480 | tf_op jit(solution)/shard_map/rjch,rjcd->jhd/dot_general | solution.py:69
  165.3 8.4 %copy.90 = bf16[2,180,2880]{1,0,2:T(2,128)(2,1)} copy(bf16[2,180,2880]{2,1,0:T(8,128)(2,1)} %fusion.25) | data formatting | bytes 4147200
  173.7 7.4 %reshape.74 = bf16[2880,360]{1,0:T(8,128)(2,1)} reshape(bf16[2880,2,180]{2,1,0:T(2,128)(2,1)} %bitcast.59) | data formatting | bytes 4147200
  181.1 0.0 reduce-scatter.15.cloned.1.call-update
  181.1 0.0 reduce-scatter.13.cloned.1.call-start
  181.2 5.7 %fusion.28 = bf16[2,180,2880]{2,1,0:T(8,128)(2,1)} fusion(bf16[64,2,8,2880]{3,2,1,0:T(8,128)(2,1)} %get-tuple-element.17, bf16[64,2,8,180]{3,2,0,1:T(8,128)(2,1)S(1)} %get-tuple-element.19), kind=kOutput, calls=%fused_computation.21 | convolution fusion | flops 1062720000 | bytes 8340480 | tf_op jit(solution)/shard_map/rjch,rjcd->jhd/dot_general | solution.py:66
  186.9 8.4 %copy.88 = bf16[2,180,2880]{1,0,2:T(2,128)(2,1)} copy(bf16[2,180,2880]{2,1,0:T(8,128)(2,1)} %fusion.28) | data formatting | bytes 4147200
  195.3 0.0 copy-start.1
  195.3 7.6 %reshape.72 = bf16[2880,360]{1,0:T(8,128)(2,1)} reshape(bf16[2880,2,180]{2,1,0:T(2,128)(2,1)} %bitcast.60) | data formatting | bytes 4147200
  202.9 0.0 reduce-scatter.13.cloned.1.call-update
  202.9 0.0 reduce-scatter.11.cloned.1.call-done
  203.0 4.0 %all-to-all-start.1 = ((bf16[4,16,2880]{2,1,0:T(8,128)(2,1)}), bf16[4,16,2880]{2,1,0:T(8,128)(2,1)S(1)}, u32[]{:S(2)}, u32[]{:S(2)}) async-start(bf16[4,16,2880]{2,1,0:T(8,128)(2,1)} %bitcast.69), calls=%async_computation.2 | async-start | bytes 753664 | tf_op jit(solution)/shard_map/all_to_all | solution.py:87
  207.0 29.6 %reduce-scatter.17.cloned.1.call-done = bf16[720,360]{1,0:T(8,128)(2,1)} async-done(((bf16[2880,360]{1,0:T(8,128)(2,1)}), bf16[720,360]{1,0:T(8,128)(2,1)}) %reduce-scatter.17.cloned.1.call-update) | async-done | bytes 518416
  236.5 2.5 reshape.77
  239.1 2.5 copy.69
  241.6 30.4 %reduce-scatter.15.cloned.1.call-done = bf16[720,360]{1,0:T(8,128)(2,1)} async-done(((bf16[2880,360]{1,0:T(8,128)(2,1)}), bf16[720,360]{1,0:T(8,128)(2,1)}) %reduce-scatter.15.cloned.1.call-update) | async-done | bytes 518416
  272.0 2.5 reshape.75
  274.5 2.5 copy.68
  277.1 30.4 %reduce-scatter.13.cloned.1.call-done = bf16[720,360]{1,0:T(8,128)(2,1)} async-done(((bf16[2880,360]{1,0:T(8,128)(2,1)}), bf16[720,360]{1,0:T(8,128)(2,1)}) %reduce-scatter.13.cloned.1.call-update) | async-done | bytes 518416
  307.5 2.5 reshape.73
  310.0 2.5 copy.67
  312.6 0.0 all-to-all-done.1
  312.6 0.8 convolution_convert_fusion.2
  313.3 0.0 copy-done.1
  (1 shorter events, 0.0 us)
Async XLA Ops:
  7.2 115.1 %copy-start = (bf16[2,180,2880]{2,0,1:T(2,128)(2,1)S(1)}, bf16[2,180,2880]{2,0,1:T(2,128)(2,1)}, u32[]{:S(2)}) copy-start(bf16[2,180,2880]{2,0,1:T(2,128)(2,1)} %param.12) | copy-start | bytes 6220804
  7.2 97.8 %all-gather.3.cloned.1.call-start = ((), (), s32[]{:S(2)}) async-start(), calls=%async_computation.7 | async-start | bytes 12812288 | tf_op jit(solution)/shard_map/all_gather | solution.py:49
  29.2 173.7 %reduce-scatter.11.cloned.1.call-start = ((), (), s32[]{:S(2)}) async-start(), calls=%async_computation.6 | async-start | bytes 6406144 | tf_op jit(solution)/shard_map/reduce_scatter | solution.py:80
  114.7 5.3 %copy-start.2 = (bf16[64,2,8,2880]{3,2,1,0:T(8,128)(2,1)S(1)}, bf16[64,2,8,2880]{3,2,1,0:T(8,128)(2,1)}, u32[]{:S(2)}) copy-start(bf16[64,2,8,2880]{3,2,1,0:T(8,128)(2,1)} %get-tuple-element.17) | copy-start | bytes 17694724
  114.7 5.7 %copy-start.3 = (bf16[2,180,2880]{2,0,1:T(2,128)(2,1)S(1)}, bf16[2,180,2880]{2,0,1:T(2,128)(2,1)}, u32[]{:S(2)}) copy-start(bf16[2,180,2880]{2,0,1:T(2,128)(2,1)} %param.11) | copy-start | bytes 6220804
  137.1 1.0 copy-start.4
  137.2 99.4 %reduce-scatter.17.cloned.1.call-start = ((), (), s32[]{:S(2)}) async-start(), calls=%async_computation.10 | async-start | bytes 2764800
  159.6 112.4 %reduce-scatter.15.cloned.1.call-start = ((), (), s32[]{:S(2)}) async-start(), calls=%async_computation.9 | async-start | bytes 2764800
  181.1 126.3 %reduce-scatter.13.cloned.1.call-start = ((), (), s32[]{:S(2)}) async-start(), calls=%async_computation.8 | async-start | bytes 2764800
  195.3 118.0 %copy-start.1 = (bf16[2,180,2880]{2,0,1:T(2,128)(2,1)S(1)}, bf16[2,180,2880]{2,0,1:T(2,128)(2,1)}, u32[]{:S(2)}) copy-start(bf16[2,180,2880]{2,0,1:T(2,128)(2,1)} %param.12) | copy-start | bytes 6220804
  203.0 109.6 %all-to-all-start.1 = ((bf16[4,16,2880]{2,1,0:T(8,128)(2,1)}), bf16[4,16,2880]{2,1,0:T(8,128)(2,1)S(1)}, u32[]{:S(2)}, u32[]{:S(2)}) async-start(bf16[4,16,2880]{2,1,0:T(8,128)(2,1)} %bitcast.69), calls=%async_computation.2 | async-start | bytes 753664 | tf_op jit(solution)/shard_map/all_to_all | solution.py:87
Sparse Core Ops, SparseCore 0:
  29.4 75.5 all-gather.2
  137.3 61.5 reduce-scatter.10
  201.4 35.0 reduce-scatter.16
  238.9 32.9 reduce-scatter.14
  274.4 33.0 reduce-scatter.12
where the time goes:
time: 321 us; the launch traced here: 320 us
  waiting for transfers between devices  166 us (52%)
  local copies, waits for them, and re-layouts  82.2 us (26%)
  matrix products  36.9 us (11%)
  blocking collectives  15.9 us (5%)
  between operations  13.9 us (4%)
  starting transfers between devices  4.37 us (1%)
    unnamed x8, waiting for transfers between devices  90.5 us
    all_gather x1, waiting for transfers between devices, on_device(): lax.all_gather(landed.reshape(2, 1, n_group, slot_block, model_width), 'm...  75.7 us
    unnamed x24, local copies, waits for them, and re-layouts  65.7 us
    all_to_all x1, blocking collectives, on_device(): lax.all_to_all(outgoing.reshape(2, n_group, slot_block, model_width), 'gr...  15.9 us
    squeeze x1, local copies, waits for them, and re-layouts, on_device(): scaled_rows = arrived_data[1]  9.69 us
  transfers between devices with their start and end apart: 6, of which 4 were waited for; matrix products, arithmetic and copies ran while one was open for 25% of the time, Pallas kernels for 0%

commit v1 on v0

--- a/solution.py
+++ b/solution.py
@@ -46,8 +46,16 @@
         concat_axis=1,
         tiled=True,
     )
-    arrived = lax.all_gather(
-        landed.reshape(2, 1, n_group, slot_block, model_width), "member", axis=1, tiled=True
+    arrived = jnp.concatenate(
+        lax.all_to_all(
+            jnp.stack(
+                [landed.reshape(2, 1, n_group, slot_block, model_width)] * lax.axis_size("member")
+            ),
+            "member",
+            0,
+            0,
+        ),
+        axis=1,
     )
     arrived_data = arrived.reshape(2, n_member * n_group, local_experts, capacity, model_width)
     inputs_rows = arrived_data[0]

time: 321 us -> 528 us (1.64)
  blocking collectives: 15.9 us -> 291 us
  waiting for transfers between devices: 166 us -> 87.5 us
  local copies, waits for them, and re-layouts: 82.2 us -> 92.9 us
    all_to_all x0 -> x1, blocking collectives: none -> 275 us  [on_device(): lax.all_to_all(jnp.stack([landed.reshape(2, 1, n_group, slot_block, model...]
    all_gather x1 -> x0, waiting for transfers between devices: 75.7 us -> none  [on_device(): lax.all_gather(landed.reshape(2, 1, n_group, slot_block, model_width), 'm...]
    slice x0 -> x1, local copies, waits for them, and re-layouts: none -> 9.72 us  [on_device(): scaled_rows = arrived_data[1]]
    squeeze x1 -> x0, local copies, waits for them, and re-layouts: 9.69 us -> none  [on_device(): scaled_rows = arrived_data[1]]
    another operation x0 -> x1, local copies, waits for them, and re-layouts: none -> 5.88 us  [on_device(): jnp.stack([landed.reshape(2, 1, n_group, slot_block, model_width)] * lax....]
    all_to_all x0 -> x1, local copies, waits for them, and re-layouts: none -> 5.73 us  [on_device(): lax.all_to_all(jnp.stack([landed.reshape(2, 1, n_group, slot_block, model...]
    unnamed x8 -> x7, waiting for transfers between devices: 90.5 us -> 87.5 us
  transfers between devices with their start and end apart: 6 -> 5, of which waited for: 4 -> 3; matrix products, arithmetic and copies ran while one was open for 25% -> 15% of each run, Pallas kernels for 0% -> 0%
where the time goes in v1:
time: 528 us; the launch traced here: 526 us
  blocking collectives  291 us (55%)
  local copies, waits for them, and re-layouts  92.9 us (18%)
  waiting for transfers between devices  87.5 us (17%)
  matrix products  36.9 us (7%)
  between operations  13.9 us (3%)
    all_to_all x1, blocking collectives, on_device(): lax.all_to_all(jnp.stack([landed.reshape(2, 1, n_group, slot_block, model...  275 us
    unnamed x7, waiting for transfers between devices  87.5 us
    unnamed x24, local copies, waits for them, and re-layouts  65.7 us
    all_to_all x1, blocking collectives, on_device(): lax.all_to_all(outgoing.reshape(2, n_group, slot_block, model_width), 'gr...  15.9 us
  transfers between devices with their start and end apart: 5, of which 3 were waited for; matrix products, arithmetic and copies ran while one was open for 15% of the time, Pallas kernels for 0%

profile of v1, /device:TPU:1, one launch (start us, length us, event | category | flops | bytes accessed | tf_op | source)
XLA Modules:
  0.0 526.2 jit_solution(15100854044420625088)
XLA Ops:
  7.2 0.0 copy-start
  7.2 0.0 reduce-scatter.11.cloned.1.call-start
  7.2 0.9 copy.47
  8.1 0.1 reshape.56
  8.2 0.8 copy.48
  9.0 0.1 mul.50
  9.0 0.1 fusion.57
  9.1 0.1 reduce_window_sum.11
  9.2 0.2 select_reduce_fusion
  9.4 0.3 convolution_convert_fusion.3
  9.6 0.3 fusion.55
  9.9 1.3 convolution_convert_fusion
  11.2 1.1 convolution_convert_fusion.1
  12.3 0.1 pad_maximum_fusion
  12.4 15.9 %all_to_all.15 = bf16[2,4,16,2880]{3,2,0,1:T(8,128)(2,1)S(1)} all-to-all(bf16[2,4,16,2880]{3,2,0,1:T(8,128)(2,1)S(1)} %pad_maximum_fusion), channel_id=1, replica_groups=mesh['dp'=4,'group'=4,'member'=16] {'group'}, dimensions={1} | all-to-all | bytes 1474560 | tf_op jit(solution)/shard_map/all_to_all | solution.py:42
  28.3 0.1 copy.51
  28.3 5.9 %stack.15 = bf16[16,2,1,4,16,2880]{5,4,3,2,1,0:T(8,128)(2,1)} broadcast(bf16[2,4,16,2880]{3,2,1,0:T(8,128)(2,1)S(1)} %copy.51), dimensions={1,3,4,5} | broadcast | bytes 12533760 | tf_op jit(solution)/shard_map/stack | solution.py:51
  34.2 274.7 %all_to_all.16 = bf16[16,2,1,4,16,2880]{5,4,3,2,1,0:T(8,128)(2,1)S(1)} all-to-all(bf16[16,2,1,4,16,2880]{5,4,3,2,1,0:T(8,128)(2,1)} %stack.15), channel_id=1, replica_groups=mesh['dp'=4,'group'=4,'member'=16] {'member'}, dimensions={0} | all-to-all | bytes 23592960 | tf_op jit(solution)/shard_map/all_to_all | solution.py:50
  308.9 5.7 %copy.155 = bf16[16,2,1,4,16,2880]{5,4,3,0,2,1:T(8,128)(2,1)} copy(bf16[16,2,1,4,16,2880]{5,4,3,2,1,0:T(8,128)(2,1)S(1)} %all_to_all.16) | data formatting | bytes 23592960 | tf_op jit(solution)/shard_map/all_to_all | solution.py:50
  314.6 9.7 %fusion.65 = (bf16[1,16,1,4,16,2880]{5,4,3,1,2,0:T(8,128)(2,1)}, bf16[1,16,1,4,16,2880]{5,4,3,1,2,0:T(8,128)(2,1)}) fusion(bf16[2,16,1,4,16,2880]{5,4,3,1,2,0:T(8,128)(2,1)} %bitcast.58), kind=kLoop, calls=%fused_computation.61 | loop fusion | bytes 23592960 | tf_op jit(solution)/shard_map/slice | solution.py:62
  324.3 0.0 copy-start.2
  324.3 0.0 copy-start.3
  324.3 5.3 %fusion.47 = f32[64,2,8,180]{3,2,0,1:T(8,128)S(1)} fusion(bf16[2,180,2880,1]{2,0,1,3:T(2,128)(2,1)} %bitcast.78, bf16[64,2,8,2880]{3,2,1,0:T(8,128)(2,1)} %bitcast.67), kind=kOutput, calls=%fused_computation.32 | convolution fusion | flops 1061683200 | bytes 8709120 | tf_op jit(solution)/shard_map/rjcd,jhd->rjch/dot_general | solution.py:67
  329.6 0.0 copy-done.2
  329.7 0.4 copy-done.3
  330.0 1.8 fusion.42
  331.8 0.0 copy-done
  331.9 3.0 multiply_convert_fusion
  334.9 1.8 fusion.32
  336.7 4.4 fusion.12
  341.1 5.7 %copy.61 = bf16[64,2,8,2880]{3,2,1,0:T(8,128)(2,1)} copy(bf16[64,2,8,2880]{3,2,0,1:T(8,128)(2,1)} %fusion.12) | data formatting | bytes 11796480 | tf_op jit(solution)/shard_map/convert_element_type | solution.py:89
  346.8 0.0 copy-start.4
  346.8 0.0 reduce-scatter.11.cloned.1.call-update
  346.8 0.2 reduce-scatter.17.cloned.1.call-start
  347.1 0.8 copy-done.4
  347.8 5.6 %fusion.22 = bf16[2,180,2880]{2,1,0:T(8,128)(2,1)} fusion(bf16[64,2,8,2880]{3,2,1,0:T(8,128)(2,1)} %bitcast.68, bf16[64,2,8,180]{3,2,0,1:T(8,128)(2,1)S(1)} %copy-done.4), kind=kOutput, calls=%fused_computation.18 | convolution fusion | flops 1062720000 | bytes 8340480 | tf_op jit(solution)/shard_map/rjch,rjcd->jhd/dot_general | solution.py:80
  353.4 8.4 %copy.93 = bf16[2,180,2880]{1,0,2:T(2,128)(2,1)} copy(bf16[2,180,2880]{2,1,0:T(8,128)(2,1)} %fusion.22) | data formatting | bytes 4147200
  361.8 7.4 %reshape.72 = bf16[2880,360]{1,0:T(8,128)(2,1)} reshape(bf16[2880,2,180]{2,1,0:T(2,128)(2,1)} %bitcast.60) | data formatting | bytes 4147200
  369.3 0.0 reduce-scatter.17.cloned.1.call-update
  369.3 0.0 reduce-scatter.15.cloned.1.call-start
  369.3 5.6 %fusion.25 = bf16[2,180,2880]{2,1,0:T(8,128)(2,1)} fusion(bf16[64,2,8,2880]{3,2,1,0:T(8,128)(2,1)} %bitcast.63, bf16[64,2,8,180]{3,2,0,1:T(8,128)(2,1)S(1)} %get-tuple-element.20), kind=kOutput, calls=%fused_computation.19 | convolution fusion | flops 1062720000 | bytes 8340480 | tf_op jit(solution)/shard_map/rjch,rjcd->jhd/dot_general | solution.py:77
  374.9 8.4 %copy.91 = bf16[2,180,2880]{1,0,2:T(2,128)(2,1)} copy(bf16[2,180,2880]{2,1,0:T(8,128)(2,1)} %fusion.25) | data formatting | bytes 4147200
  383.4 7.4 %reshape.70 = bf16[2880,360]{1,0:T(8,128)(2,1)} reshape(bf16[2880,2,180]{2,1,0:T(2,128)(2,1)} %bitcast.61) | data formatting | bytes 4147200
  390.8 0.0 reduce-scatter.15.cloned.1.call-update
  390.8 0.0 reduce-scatter.13.cloned.1.call-start
  390.8 5.6 %fusion.28 = bf16[2,180,2880]{2,1,0:T(8,128)(2,1)} fusion(bf16[64,2,8,2880]{3,2,1,0:T(8,128)(2,1)} %bitcast.64, bf16[64,2,8,180]{3,2,0,1:T(8,128)(2,1)S(1)} %get-tuple-element.19), kind=kOutput, calls=%fused_computation.20 | convolution fusion | flops 1062720000 | bytes 8340480 | tf_op jit(solution)/shard_map/rjch,rjcd->jhd/dot_general | solution.py:74
  396.5 8.4 %copy.89 = bf16[2,180,2880]{1,0,2:T(2,128)(2,1)} copy(bf16[2,180,2880]{2,1,0:T(8,128)(2,1)} %fusion.28) | data formatting | bytes 4147200
  404.9 0.0 copy-start.1
  404.9 7.6 %reshape.68 = bf16[2880,360]{1,0:T(8,128)(2,1)} reshape(bf16[2880,2,180]{2,1,0:T(2,128)(2,1)} %bitcast.62) | data formatting | bytes 4147200
  412.5 0.0 reduce-scatter.13.cloned.1.call-update
  412.5 0.0 reduce-scatter.11.cloned.1.call-done
  412.5 3.7 all-to-all-start.2
  416.2 26.4 %reduce-scatter.17.cloned.1.call-done = bf16[720,360]{1,0:T(8,128)(2,1)} async-done(((bf16[2880,360]{1,0:T(8,128)(2,1)}), bf16[720,360]{1,0:T(8,128)(2,1)}) %reduce-scatter.17.cloned.1.call-update) | async-done | bytes 518416
  442.7 2.5 reshape.73
  445.2 2.5 copy.70
  447.7 30.6 %reduce-scatter.15.cloned.1.call-done = bf16[720,360]{1,0:T(8,128)(2,1)} async-done(((bf16[2880,360]{1,0:T(8,128)(2,1)}), bf16[720,360]{1,0:T(8,128)(2,1)}) %reduce-scatter.15.cloned.1.call-update) | async-done | bytes 518416
  478.3 2.5 reshape.71
  480.9 2.5 copy.69
  483.4 30.4 %reduce-scatter.13.cloned.1.call-done = bf16[720,360]{1,0:T(8,128)(2,1)} async-done(((bf16[2880,360]{1,0:T(8,128)(2,1)}), bf16[720,360]{1,0:T(8,128)(2,1)}) %reduce-scatter.13.cloned.1.call-update) | async-done | bytes 518416
  513.8 2.5 reshape.69
  516.4 2.5 copy.68
  518.9 0.0 all-to-all-done.2
  518.9 0.8 convolution_convert_fusion.2
  519.7 0.0 copy-done.1
  (1 shorter events, 0.0 us)
Async XLA Ops:
  7.2 324.7 %copy-start = (bf16[2,180,2880]{2,0,1:T(2,128)(2,1)S(1)}, bf16[2,180,2880]{2,0,1:T(2,128)(2,1)}, u32[]{:S(2)}) copy-start(bf16[2,180,2880]{2,0,1:T(2,128)(2,1)} %param.12) | copy-start | bytes 6220804
  7.2 405.3 %reduce-scatter.11.cloned.1.call-start = ((), (), s32[]{:S(2)}) async-start(), calls=%async_computation.7 | async-start | bytes 6406144 | tf_op jit(solution)/shard_map/reduce_scatter | solution.py:88
  324.3 5.3 %copy-start.2 = (bf16[1,16,1,4,16,2880]{5,4,3,1,2,0:T(8,128)(2,1)S(1)}, bf16[1,16,1,4,16,2880]{5,4,3,1,2,0:T(8,128)(2,1)}, u32[]{:S(2)}) copy-start(bf16[1,16,1,4,16,2880]{5,4,3,1,2,0:T(8,128)(2,1)} %get-tuple-element.17) | copy-start | bytes 17694724
  324.3 5.7 %copy-start.3 = (bf16[2,180,2880]{2,0,1:T(2,128)(2,1)S(1)}, bf16[2,180,2880]{2,0,1:T(2,128)(2,1)}, u32[]{:S(2)}) copy-start(bf16[2,180,2880]{2,0,1:T(2,128)(2,1)} %param.11) | copy-start | bytes 6220804
  346.8 1.0 copy-start.4
  346.8 95.9 %reduce-scatter.17.cloned.1.call-start = ((), (), s32[]{:S(2)}) async-start(), calls=%async_computation.10 | async-start | bytes 2764800
  369.3 109.0 %reduce-scatter.15.cloned.1.call-start = ((), (), s32[]{:S(2)}) async-start(), calls=%async_computation.9 | async-start | bytes 2764800
  390.8 123.0 %reduce-scatter.13.cloned.1.call-start = ((), (), s32[]{:S(2)}) async-start(), calls=%async_computation.8 | async-start | bytes 2764800
  404.9 114.8 %copy-start.1 = (bf16[2,180,2880]{2,0,1:T(2,128)(2,1)S(1)}, bf16[2,180,2880]{2,0,1:T(2,128)(2,1)}, u32[]{:S(2)}) copy-start(bf16[2,180,2880]{2,0,1:T(2,128)(2,1)} %param.12) | copy-start | bytes 6220804
  412.5 106.4 %all-to-all-start.2 = ((bf16[4,16,2880]{2,1,0:T(8,128)(2,1)}), bf16[4,16,2880]{2,1,0:T(8,128)(2,1)S(1)}, u32[]{:S(2)}, u32[]{:S(2)}) async-start(bf16[4,16,2880]{2,1,0:T(8,128)(2,1)} %bitcast.77), calls=%async_computation.3 | async-start | bytes 753664 | tf_op jit(solution)/shard_map/all_to_all | solution.py:95
Sparse Core Ops, SparseCore 0:
  346.9 58.3 reduce-scatter.10
  407.9 34.7 reduce-scatter.16
  445.3 33.0 reduce-scatter.14
  480.8 33.0 reduce-scatter.12
